TPU v7x, 128 devices: a whole 4x4x4 slice. The times are simulated.
128 devices in a mesh: seq: 8 (over x, core), chan: 16 (over y, z).
Axes of the slice: x: 4, y: 4, z: 4, core: 2. Of those that a mesh axis runs over, the one named last changes fastest.
Arguments:
- tokens: bfloat16 [6144, 8192], P('seq', 'chan'), may hold values from -6 to 6
- norm_gain: bfloat16 [8192], P('chan'), may hold values from 0.099609375 to 1.8984375
- in_weight: bfloat16 [8192, 3, 8192], P('seq', None, 'chan'), may hold values from -0.0625 to 0.0625
- conv_weight: bfloat16 [3, 3, 8192], P(None, None, 'chan'), may hold values from -3 to 3
- filters: bfloat16 [512, 128], P('chan'), may hold values from -0.5 to 0.5
- out_weight: bfloat16 [8192, 8192], P('chan'), may hold values from -0.09375 to 0.09375
Outputs:
- result: bfloat16 [6144, 8192], P('seq', 'chan')
All inputs are finite; a program needn't handle non-finite values.
Results may differ from a plain program's by a relative error of at most 0.0084.
Values may be sent and summed in bfloat16 or wider, within the bound.
A program may use at most 192 MiB of HBM per device.

v0:
```python
import jax
import jax.numpy as jnp
import numpy as np
from jax import lax
from jax.sharding import PartitionSpec as P


def lag_table(filters):
    groups, length = filters.shape
    width = 3 * length
    zeros = jnp.zeros((groups, length), filters.dtype)
    skew = jnp.concatenate([zeros, filters[:, ::-1], zeros], axis=1)
    tiled = jnp.tile(skew, (1, length + 1))[:, : length * (width + 1)]
    windows = tiled.reshape(groups, length, width + 1)[:, :, : 2 * length]
    return windows[:, ::-1, :]


def hyena_core(extended, conv_weight, filters):
    length = filters.shape[1]
    values = extended.astype(jnp.float32)
    weights = conv_weight.astype(jnp.float32)
    shaped = (
        weights[:, 0, :] * values[2:]
        + weights[:, 1, :] * values[1:-1]
        + weights[:, 2, :] * values[:-2]
    )
    total = shaped.shape[0]
    out_rows = total - length
    query = shaped[length:, 0, :]
    mixed = (shaped[:, 1, :] * shaped[:, 2, :]).astype(jnp.bfloat16)
    group_count = filters.shape[0]
    channel_count = mixed.shape[1]
    blocks = mixed.reshape(total // length, length, group_count, channel_count // group_count)
    paired = jnp.concatenate([blocks[:-1], blocks[1:]], axis=1)
    table = lag_table(filters)
    filtered = jnp.einsum("gts,bsgw->btgw", table, paired, preferred_element_type=jnp.float32)
    filtered = filtered.reshape(out_rows, channel_count)
    return (query * filtered).astype(jnp.bfloat16)


def local(tokens, norm_gain, in_weight, conv_weight, filters, out_weight):
    row_count = tokens.shape[0]
    chan_count = in_weight.shape[2]
    length = filters.shape[1]
    joined = jnp.concatenate([tokens, norm_gain[None, :]], axis=0)
    whole_joined = lax.all_gather(joined, "chan", axis=1, tiled=True)
    whole, gain_whole = (whole_joined[:row_count], whole_joined[row_count])
    values = whole.astype(jnp.float32)
    mean_square = jnp.mean(values * values, axis=1, keepdims=True)
    normed = (values * lax.rsqrt(mean_square + 1e-06) * gain_whole.astype(jnp.float32)).astype(
        jnp.bfloat16
    )
    piece = lax.all_gather(in_weight, "seq", axis=0, tiled=True)
    panel = piece.reshape(piece.shape[0], 3 * chan_count)
    projected = jnp.dot(normed, panel, preferred_element_type=jnp.float32)
    streams = projected.astype(jnp.bfloat16).reshape(row_count, 3, chan_count)
    parts_count = lax.axis_size("seq")
    halo_rows = length + 2
    shift = [(i, i + 1) for i in range(parts_count - 1)]
    halo = lax.ppermute(streams[row_count - halo_rows :], "seq", shift)
    extended = jnp.concatenate([halo, streams], axis=0)
    gated = hyena_core(extended, conv_weight, filters)
    partial_out = jnp.dot(gated, out_weight, preferred_element_type=jnp.float32)
    summed = lax.psum_scatter(partial_out, "chan", scatter_dimension=1, tiled=True)
    return (tokens.astype(jnp.float32) + summed).astype(jnp.bfloat16)


def solution(mesh):
    return jax.shard_map(
        local,
        mesh=mesh,
        in_specs=(
            P("seq", "chan"),
            P("chan"),
            P("seq", None, "chan"),
            P(None, None, "chan"),
            P("chan", None),
            P("chan", None),
        ),
        out_specs=P("seq", "chan"),
        check_vma=False,
    )
```

profile of v0, /device:TPU:1, one launch (start us, length us, event | category | flops | bytes accessed | tf_op | source)
XLA Modules:
  0.0 496.6 jit_solution(15601686603221840330)
XLA Ops:
  6.5 0.7 broadcast_in_dim.8
  7.2 2.1 pad_maximum_fusion
  9.4 4.6 copy.13
  14.1 96.5 %all-gather.3.cloned.1.call-done = bf16[769,8192]{1,0:T(8,128)(2,1)} async-done(((bf16[769,512]{1,0:T(8,128)(2,1)}), bf16[769,8192]{1,0:T(8,128)(2,1)}) %all-gather.3.cloned.1.call-update) | async-done | bytes 12599312 | tf_op jit(solution)/shard_map/all_gather | solution.py:46
  110.6 7.1 %fusion = f32[768]{0:T(1024)S(1)} fusion(bf16[769,8192]{1,0:T(8,128)(2,1)} %all-gather.3.cloned.1.call-done), kind=kLoop, calls=%fused_computation.2 | loop fusion | flops 18873600 | bytes 12585984 | tf_op jit(solution)/shard_map/reduce_sum | solution.py:49
  117.7 0.9 slice_convert_fusion
  118.7 114.9 %all-gather.5.cloned.1.call-done = bf16[8192,3,512]{0,2,1:T(8,128)(2,1)} async-done(((bf16[1024,3,512]{0,2,1:T(8,128)(2,1)}), bf16[8192,3,512]{0,2,1:T(8,128)(2,1)}) %all-gather.5.cloned.1.call-update) | async-done | bytes 25165840 | tf_op jit(solution)/shard_map/all_gather | solution.py:53
  233.5 27.1 %fusion.10 = bf16[768,1536]{1,0:T(8,128)(2,1)S(1)} fusion(bf16[8192,1536]{0,1:T(8,128)(2,1)} %bitcast.49, f32[8192]{0:T(1024)S(1)} %bitcast.48, f32[768]{0:T(1024)S(1)} %add_rsqrt_fusion, bf16[769,8192]{1,0:T(8,128)(2,1)} %all-gather.3.cloned.1.call-done), kind=kOutput, calls=%fused_computation.14 | convolution fusion | flops 19353698304 | bytes 40143872 | tf_op jit(solution)/shard_map/dot_general | solution.py:55
  260.8 0.3 slice.63
  261.1 1.1 copy.14
  262.2 3.4 collective-permute-start
  265.7 0.3 tile.4
  266.0 0.4 copy.24
  266.5 0.2 slice.92
  266.7 8.9 %reshape.39 = bf16[32,128,385]{2,1,0:T(8,128)(2,1)} reshape(bf16[32,49280]{1,0:T(8,128)(2,1)S(1)} %slice.92) | data formatting | bytes 6307840 | tf_op jit(solution)/shard_map/reshape | solution.py:14
  275.6 1.6 slice-done.2
  277.2 20.2 %rev.7 = bf16[32,128,256]{2,1,0:T(8,128)(2,1)} reverse(bf16[32,128,256]{2,1,0:T(8,128)(2,1)S(1)} %slice-done.2), dimensions={1} | reverse | bytes 4194304 | tf_op jit(solution)/shard_map/rev | solution.py:15
  297.4 2.8 copy.15
  300.3 1.3 copy.16
  301.6 1.3 maximum_convert_fusion
  302.9 4.5 fusion.8
  307.4 2.4 copy-done
  309.8 0.2 fusion.15
  310.0 1.3 fusion.28
  311.3 2.0 slice.73
  313.2 1.0 copy.17
  314.3 2.0 slice.75
  316.4 2.1 fusion.20
  318.5 0.6 copy.19
  319.1 15.5 %fusion.25 = f32[768,8192]{1,0:T(8,128)} fusion(bf16[512,8192]{1,0:T(8,128)(2,1)} %param.11, f32[64,8,6,128]{3,2,1,0:T(8,128)S(1)} %bitcast.44, f32[896,3,512]{0,2,1:T(8,128)S(1)} %bitcast.42), kind=kOutput, calls=%fused_computation.29 | convolution fusion | flops 6443237376 | bytes 37224448 | tf_op jit(solution)/shard_map/dot_general | solution.py:63
  334.6 152.9 %reduce-scatter.2.cloned.1.call-done = f32[768,512]{1,0:T(8,128)} async-done(((f32[768,8192]{1,0:T(8,128)}), f32[768,512]{1,0:T(8,128)}) %reduce-scatter.2.cloned.1.call-update) | async-done | bytes 1572880 | tf_op jit(solution)/shard_map/reduce_scatter | solution.py:64
  487.5 2.5 add_convert_fusion
  (33 shorter events, 0.5 us)
Async XLA Ops:
  6.5 104.1 %all-gather.3.cloned.1.call-start = ((), (), s32[]{:S(2)}) async-start(), calls=%async_computation.1 | async-start | bytes 13508608 | tf_op jit(solution)/shard_map/all_gather | solution.py:46
  9.3 224.2 %all-gather.5.cloned.1.call-start = ((), (), s32[]{:S(2)}) async-start(), calls=%async_computation.2 | async-start | bytes 28311552 | tf_op jit(solution)/shard_map/all_gather | solution.py:53
  14.1 473.4 %reduce-scatter.2.cloned.1.call-start = ((), (), s32[]{:S(2)}) async-start(), calls=%async_computation.3 | async-start | bytes 26738688 | tf_op jit(solution)/shard_map/reduce_scatter | solution.py:64
  233.5 32.1 %copy-start.4 = (bf16[3,3,512]{2,1,0:T(4,128)(2,1)S(1)}, bf16[3,3,512]{2,1,0:T(4,128)(2,1)}, u32[]{:S(2)}) copy-start(bf16[3,3,512]{2,1,0:T(4,128)(2,1)} %param.9) | copy-start | bytes 27652
  233.5 32.1 %copy-start.5 = (bf16[32,128]{1,0:T(8,128)(2,1)S(1)}, bf16[32,128]{1,0:T(8,128)(2,1)}, u32[]{:S(2)}) copy-start(bf16[32,128]{1,0:T(8,128)(2,1)} %param.10) | copy-start | bytes 24580
  260.7 5.8 %copy-start.2 = (bf16[768,1536]{1,0:T(8,128)(2,1)}, bf16[768,1536]{1,0:T(8,128)(2,1)S(1)}, u32[]{:S(2)}) copy-start(bf16[768,1536]{1,0:T(8,128)(2,1)S(1)} %fusion.10) | copy-start | bytes 7077892
  262.2 38.1 %collective-permute-start = (bf16[130,3,512]{2,0,1:T(8,128)(2,1)}, bf16[130,3,512]{2,0,1:T(8,128)(2,1)}, u32[]{:S(2)}, u32[]{:S(2)}) collective-permute-start(bf16[130,3,512]{2,0,1:T(8,128)(2,1)} %copy.14), channel_id=1, source_target_pairs={{0,16},{16,32},{32,48},{48,64},{64,80},{80,96},{96,112},{1,17},{17... | collective-permute-start | bytes 1198088 | tf_op jit(solution)/shard_map/ppermute | solution.py:60
  275.6 1.6 slice-start.2
  307.4 2.4 copy-start
  310.0 6.4 %copy-start.1 = (bf16[32,128,256]{2,1,0:T(8,128)(2,1)S(1)}, bf16[32,128,256]{2,1,0:T(8,128)(2,1)}, u32[]{:S(2)}) copy-start(bf16[32,128,256]{2,1,0:T(8,128)(2,1)} %rev.7) | copy-start | bytes 6291460
  316.2 2.9 slice-start
  316.4 2.7 slice-start.1
  334.6 152.9 %copy-start.3 = (bf16[768,512]{1,0:T(8,128)(2,1)S(1)}, bf16[768,512]{1,0:T(8,128)(2,1)}, u32[]{:S(2)}) copy-start(bf16[768,512]{1,0:T(8,128)(2,1)} %param.6) | copy-start | bytes 2359300
Sparse Core Ops, SparseCore 0:
  9.5 101.1 all-gather.2
  112.3 121.1 all-gather.4
  334.8 152.6 reduce-scatter.1
where the time goes:
time: 497 us
  waiting for transfers between devices  364 us (73%)
  local copies, waits for them, and re-layouts  52.1 us (10%)
  matrix products  44.7 us (9%)
  other arithmetic  18.7 us (4%)
  between operations  13.4 us (3%)
    reduce_scatter x1, waiting for transfers between devices, local(): lax.psum_scatter(partial_out, 'chan', scatter_dimension=1, tiled=True)  153 us
    all_gather x1, waiting for transfers between devices, local(): piece = lax.all_gather(in_weight, 'seq', axis=0, tiled=True)  115 us
    all_gather x1, waiting for transfers between devices, local(): whole_joined = lax.all_gather(joined, 'chan', axis=1, tiled=True)  96.5 us
    dot_general x1, matrix products, local(): projected = jnp.dot(normed, panel, preferred_element_type=jnp.float32)  27.1 us
    rev x1, local copies, waits for them, and re-layouts, lag_table(): return windows[:, ::-1, :]  20.2 us
    dot_general x1, matrix products, local(): partial_out = jnp.dot(gated, out_weight, preferred_element_type=jnp.float32)  15.5 us
  transfers between devices with their start and end apart: 4, of which 3 were waited for; matrix products, arithmetic and copies ran while one was open for 9% of the time, Pallas kernels for 0%

commit v1 on v0

--- a/solution.py
+++ b/solution.py
@@ -3,6 +3,14 @@
 import numpy as np
 from jax import lax
 from jax.sharding import PartitionSpec as P
+
+
+def report_the_arrays(arr, row_axis, dim_i):
+    response = lax.axis_size(row_axis)
+    front = jnp.stack(response * [arr])
+    s_next = lax.all_to_all(front, axis_name=row_axis, split_axis=0, concat_axis=0)
+    e_next = jnp.concatenate(s_next, axis=dim_i)
+    return e_next
 
 
 def lag_table(filters):
@@ -50,7 +58,7 @@
     normed = (values * lax.rsqrt(mean_square + 1e-06) * gain_whole.astype(jnp.float32)).astype(
         jnp.bfloat16
     )
-    piece = lax.all_gather(in_weight, "seq", axis=0, tiled=True)
+    piece = report_the_arrays(in_weight, "seq", 0)
     panel = piece.reshape(piece.shape[0], 3 * chan_count)
     projected = jnp.dot(normed, panel, preferred_element_type=jnp.float32)
     streams = projected.astype(jnp.bfloat16).reshape(row_count, 3, chan_count)

time: 497 us -> 589 us (1.19)
  local copies, waits for them, and re-layouts: 52.1 us -> 101 us
  waiting for transfers between devices: 364 us -> 399 us
  starting transfers between devices: 3.48 us -> 11 us
    all_to_all x0 -> x1, waiting for transfers between devices: none -> 242 us  [report_the_arrays(): lax.all_to_all(front, axis_name=row_axis, split_axis=0, concat_axis=0)]
    all_gather x1 -> x0, waiting for transfers between devices: 115 us -> none  [local(): piece = lax.all_gather(in_weight, 'seq', axis=0, tiled=True)]
    all_gather x1, waiting for transfers between devices: 96.5 us -> 0.01 us  [local(): whole_joined = lax.all_gather(joined, 'chan', axis=1, tiled=True)]
    all_to_all x0 -> x1, local copies, waits for them, and re-layouts: none -> 22.4 us  [report_the_arrays(): lax.all_to_all(front, axis_name=row_axis, split_axis=0, concat_axis=0)]
    unnamed x20 -> x21, local copies, waits for them, and re-layouts: 7.5 us -> 26.3 us
    another operation x0 -> x1, local copies, waits for them, and re-layouts: none -> 8.66 us  [report_the_arrays(): front = jnp.stack(response * [arr])]
    all_to_all x0 -> x1, starting transfers between devices: none -> 7.98 us  [report_the_arrays(): lax.all_to_all(front, axis_name=row_axis, split_axis=0, concat_axis=0)]
  transfers between devices with their start and end apart: 4 -> 4, of which waited for: 3 -> 3; matrix products, arithmetic and copies ran while one was open for 9% -> 15% of each run, Pallas kernels for 0% -> 0%
where the time goes in v1:
time: 589 us; the launch traced here: 588 us
  waiting for transfers between devices  399 us (68%)
  local copies, waits for them, and re-layouts  101 us (17%)
  matrix products  44.6 us (8%)
  other arithmetic  18.6 us (3%)
  between operations  13.7 us (2%)
  starting transfers between devices  11 us (2%)
    all_to_all x1, waiting for transfers between devices, report_the_arrays(): lax.all_to_all(front, axis_name=row_axis, split_axis=0, concat_axis=0)  242 us
    reduce_scatter x1, waiting for transfers between devices, local(): lax.psum_scatter(partial_out, 'chan', scatter_dimension=1, tiled=True)  156 us
    dot_general x1, matrix products, local(): projected = jnp.dot(normed, panel, preferred_element_type=jnp.float32)  27.3 us
    unnamed x21, local copies, waits for them, and re-layouts  26.3 us
    all_to_all x1, local copies, waits for them, and re-layouts, report_the_arrays(): lax.all_to_all(front, axis_name=row_axis, split_axis=0, concat_axis=0)  22.4 us
    rev x1, local copies, waits for them, and re-layouts, lag_table(): return windows[:, ::-1, :]  20.3 us
    dot_general x1, matrix products, local(): partial_out = jnp.dot(gated, out_weight, preferred_element_type=jnp.float32)  15.3 us
  transfers between devices with their start and end apart: 4, of which 3 were waited for; matrix products, arithmetic and copies ran while one was open for 15% of the time, Pallas kernels for 0%

profile of v1, /device:TPU:1, one launch (start us, length us, event | category | flops | bytes accessed | tf_op | source)
XLA Modules:
  0.0 588.3 jit_solution(15304223125656335441)
XLA Ops:
  6.5 0.7 broadcast_in_dim.8
  7.2 2.1 pad_maximum_fusion
  9.3 3.2 copy.14
  12.5 8.7 %stack.2 = bf16[8,1024,3,512]{1,3,2,0:T(8,128)(2,1)} broadcast(bf16[1024,3,512]{0,2,1:T(8,128)(2,1)S(1)} %copy.14), dimensions={1,2,3} | broadcast | bytes 28311552 | tf_op jit(solution)/shard_map/stack | solution.py:10
  21.2 8.0 %all-to-all-start = ((bf16[8,1024,3,512]{1,3,2,0:T(8,128)(2,1)}), bf16[8,1024,3,512]{1,3,2,0:T(8,128)(2,1)}, u32[]{:S(2)}, u32[]{:S(2)}) async-start(bf16[8,1024,3,512]{1,3,2,0:T(8,128)(2,1)} %stack.2), calls=%async_computation | async-start | bytes 50331648 | tf_op jit(solution)/shard_map/all_to_all | solution.py:11
  29.6 0.4 copy.27
  30.2 8.9 %reshape.37 = bf16[32,128,385]{2,1,0:T(8,128)(2,1)} reshape(bf16[32,49280]{1,0:T(8,128)(2,1)S(1)} %slice.92) | data formatting | bytes 6307840 | tf_op jit(solution)/shard_map/reshape | solution.py:22
  39.1 1.6 slice-done.2
  40.7 20.3 %rev.7 = bf16[32,128,256]{2,1,0:T(8,128)(2,1)} reverse(bf16[32,128,256]{2,1,0:T(8,128)(2,1)S(1)} %slice-done.2), dimensions={1} | reverse | bytes 4194304 | tf_op jit(solution)/shard_map/rev | solution.py:23
  61.0 241.6 %all-to-all-done = bf16[8,1024,3,512]{1,3,2,0:T(8,128)(2,1)} async-done(((bf16[8,1024,3,512]{1,3,2,0:T(8,128)(2,1)}), bf16[8,1024,3,512]{1,3,2,0:T(8,128)(2,1)}, u32[]{:S(2)}, u32[]{:S(2)}) %all-to-all-start) | async-done | bytes 25165856 | tf_op jit(solution)/shard_map/all_to_all | solution.py:11
  302.7 22.4 %copy.15 = bf16[8,1024,3,512]{1,0,3,2:T(8,128)(2,1)S(1)} copy(bf16[8,1024,3,512]{1,3,2,0:T(8,128)(2,1)} %all-to-all-done) | data formatting | bytes 50331648 | tf_op jit(solution)/shard_map/all_to_all | solution.py:11
  325.0 20.2 %copy.26 = bf16[192,8,8,1024]{3,1,2,0:T(8,128)(2,1)} copy(bf16[192,8,8,1024]{3,2,1,0:T(8,128)(2,1)S(1)} %bitcast.45) | data formatting | bytes 50331648
  345.3 7.1 %fusion = f32[768]{0:T(1024)S(1)} fusion(bf16[769,8192]{1,0:T(8,128)(2,1)} %all-gather.2.cloned.1.call-done), kind=kLoop, calls=%fused_computation.2 | loop fusion | flops 18873600 | bytes 12585984 | tf_op jit(solution)/shard_map/reduce_sum | solution.py:57
  352.4 0.9 slice_convert_fusion
  353.3 27.3 %fusion.10 = bf16[768,1536]{1,0:T(8,128)(2,1)S(1)} fusion(bf16[8192,1536]{0,1:T(8,128)(2,1)} %bitcast.48, f32[8192]{0:T(1024)S(1)} %bitcast.54, f32[768]{0:T(1024)S(1)} %add_rsqrt_fusion, bf16[769,8192]{1,0:T(8,128)(2,1)} %all-gather.2.cloned.1.call-done), kind=kOutput, calls=%fused_computation.14 | convolution fusion | flops 19353698304 | bytes 40143872 | tf_op jit(solution)/shard_map/dot_general | solution.py:63
  380.7 0.3 slice.63
  381.1 3.0 collective-permute-start
  384.3 3.1 copy.17
  387.3 1.8 collective-permute-done
  389.2 1.3 copy.18
  390.4 1.3 maximum_convert_fusion
  391.7 4.5 fusion.8
  396.3 2.4 copy-done
  398.9 1.3 fusion.28
  400.2 2.0 slice.75
  402.1 1.0 copy.20
  403.2 2.0 slice.73
  405.3 2.1 fusion.20
  407.4 0.6 copy.21
  408.0 15.3 %fusion.25 = f32[768,8192]{1,0:T(8,128)} fusion(bf16[512,8192]{1,0:T(8,128)(2,1)} %param.11, f32[64,8,6,128]{3,2,1,0:T(8,128)S(1)} %bitcast.50, f32[896,3,512]{0,2,1:T(8,128)S(1)} %bitcast.47), kind=kOutput, calls=%fused_computation.29 | convolution fusion | flops 6443237376 | bytes 37224448 | tf_op jit(solution)/shard_map/dot_general | solution.py:71
  423.3 155.6 %reduce-scatter.2.cloned.1.call-done = f32[768,512]{1,0:T(8,128)} async-done(((f32[768,8192]{1,0:T(8,128)}), f32[768,512]{1,0:T(8,128)}) %reduce-scatter.2.cloned.1.call-update) | async-done | bytes 1572880 | tf_op jit(solution)/shard_map/reduce_scatter | solution.py:72
  578.9 2.5 add_convert_fusion
  (35 shorter events, 1.2 us)
Async XLA Ops:
  6.5 338.7 %all-gather.2.cloned.1.call-start = ((), (), s32[]{:S(2)}) async-start(), calls=%async_computation.2 | async-start | bytes 13508608 | tf_op jit(solution)/shard_map/all_gather | solution.py:54
  21.2 8.0 %copy-start.5 = (bf16[32,128]{1,0:T(8,128)(2,1)S(1)}, bf16[32,128]{1,0:T(8,128)(2,1)}, u32[]{:S(2)}) copy-start(bf16[32,128]{1,0:T(8,128)(2,1)} %param.10) | copy-start | bytes 24580
  21.2 281.5 %all-to-all-start = ((bf16[8,1024,3,512]{1,3,2,0:T(8,128)(2,1)}), bf16[8,1024,3,512]{1,3,2,0:T(8,128)(2,1)}, u32[]{:S(2)}, u32[]{:S(2)}) async-start(bf16[8,1024,3,512]{1,3,2,0:T(8,128)(2,1)} %stack.2), calls=%async_computation | async-start | bytes 50331648 | tf_op jit(solution)/shard_map/all_to_all | solution.py:11
  29.1 549.8 %reduce-scatter.2.cloned.1.call-start = ((), (), s32[]{:S(2)}) async-start(), calls=%async_computation.3 | async-start | bytes 26738688 | tf_op jit(solution)/shard_map/reduce_scatter | solution.py:72
  39.1 1.6 slice-start.2
  353.3 30.9 %copy-start.4 = (bf16[3,3,512]{2,1,0:T(4,128)(2,1)S(1)}, bf16[3,3,512]{2,1,0:T(4,128)(2,1)}, u32[]{:S(2)}) copy-start(bf16[3,3,512]{2,1,0:T(4,128)(2,1)} %param.9) | copy-start | bytes 27652
  380.6 3.6 copy-start.2
  381.1 8.0 %collective-permute-start = (bf16[130,3,512]{2,0,1:T(8,128)(2,1)S(1)}, bf16[130,3,512]{2,0,1:T(8,128)(2,1)}, u32[]{:S(2)}, u32[]{:S(2)}) collective-permute-start(bf16[130,3,512]{2,0,1:T(8,128)(2,1)S(1)} %copy.16), channel_id=1, source_target_pairs={{0,16},{16,32},{32,48},{48,64},{64,80},{80,96},{96,112},{1,17},{17... | collective-permute-start | bytes 1198088 | tf_op jit(solution)/shard_map/ppermute | solution.py:68
  396.3 2.4 copy-start
  398.9 6.4 %copy-start.1 = (bf16[32,128,256]{2,1,0:T(8,128)(2,1)S(1)}, bf16[32,128,256]{2,1,0:T(8,128)(2,1)}, u32[]{:S(2)}) copy-start(bf16[32,128,256]{2,1,0:T(8,128)(2,1)} %rev.7) | copy-start | bytes 6291460
  405.1 2.9 slice-start
  405.3 2.7 slice-start.1
  423.3 155.6 %copy-start.3 = (bf16[768,512]{1,0:T(8,128)(2,1)S(1)}, bf16[768,512]{1,0:T(8,128)(2,1)}, u32[]{:S(2)}) copy-start(bf16[768,512]{1,0:T(8,128)(2,1)} %param.6) | copy-start | bytes 2359300
Sparse Core Ops, SparseCore 0:
  9.4 101.1 all-gather.1
  423.4 155.4 reduce-scatter.1
